TPU v7x, 128 devices: a whole 4x4x4 slice. The times are simulated.
128 devices in a mesh: space: 16 (over z, x_lo, core), samp: 8 (over y, x_hi).
Axes of the slice: x: 4 (x_hi: 2, x_lo: 2; x = x_hi * 2 + x_lo), y: 4, z: 4, core: 2. Of those that a mesh axis runs over, the one named last changes fastest.
Arguments:
- basis_u: bfloat16 [128, 32, 8, 128], P('samp', 'space'), may hold values from -0.75 to 0.75
- basis_v: bfloat16 [128, 65536], P('space', 'samp'), may hold values from -0.75 to 0.75
- core_s: float32 [128, 128], replicated, may hold values from -4 to 4
- face_class: int32 [6, 32, 8, 128], P(None, 'space'), may hold values from 0 to 3
- sample_class: int32 [65536], P('samp'), may hold values from 0 to 3
Outputs:
- k_new: float32 [128, 32, 8, 128], P('samp', 'space')
- l_new: float32 [128, 65536], P('space', 'samp')
All inputs are finite; a program needn't handle non-finite values.
Results may differ from a plain program's by a relative error of at most 0.0046.
Values may be sent and summed in bfloat16 or wider, within the bound.
No kernel may reach another device: no remote copies, remote signals or barrier semaphores. Data moves between devices by JAX's collectives and lax.ppermute only.
A program may use at most 64 MiB of HBM per device.

v0:
```python
import jax
import jax.numpy as jnp
from jax import lax
from jax.sharding import PartitionSpec as P

step_size = 0.1


def padded(cells, sides, width):
    for axis, dim in sides:
        count = lax.axis_size(axis)
        ends = count - 1
        head = lax.slice_in_dim(cells, 0, width, axis=dim)
        tail = lax.slice_in_dim(cells, cells.shape[dim] - width, cells.shape[dim], axis=dim)
        cells = jnp.concatenate(
            [
                lax.ppermute(tail, axis, [(i, (i + 1) % count) for i in range(ends)]),
                cells,
                lax.ppermute(head, axis, [((i + 1) % count, i) for i in range(ends)]),
            ],
            axis=dim,
        )
    return cells


def with_core(factor, core_b):
    rank_size = core_b.shape[0]
    flat_rows = factor.reshape(rank_size, -1)
    product = lax.dot_general(
        core_b, flat_rows, (((0,), (0,)), ((), ())), preferred_element_type=jnp.float32
    ).astype(jnp.bfloat16)
    return product.reshape(factor.shape)


def diffuse(padded_k, face_class):
    weight = 0.25 * jnp.exp2(face_class.astype(jnp.float32))[:, None]
    padded_grid = jnp.pad(padded_k.astype(jnp.float32), ((0, 0), (0, 0), (1, 1), (1, 1)))
    centre = padded_grid[:, 1:-1, 1:-1, 1:-1]
    beside_all = (
        padded_grid[:, :-2, 1:-1, 1:-1],
        padded_grid[:, 2:, 1:-1, 1:-1],
        padded_grid[:, 1:-1, :-2, 1:-1],
        padded_grid[:, 1:-1, 2:, 1:-1],
        padded_grid[:, 1:-1, 1:-1, :-2],
        padded_grid[:, 1:-1, 1:-1, 2:],
    )
    summed = jnp.zeros_like(centre)
    for side_index in range(6):
        summed = summed + weight[side_index] * (beside_all[side_index] - centre)
    return summed


def per_device(basis_u, basis_v, core_s, face_class, sample_class):
    n_space = lax.axis_size("space")
    n_samp = lax.axis_size("samp")
    narrow, depth_x, rows_y, cols_z = basis_u.shape
    rank_size = core_s.shape[0]
    core_b = core_s.astype(jnp.bfloat16)
    full_u = lax.all_gather(basis_u, "samp", axis=0, tiled=True)
    k_old = with_core(full_u, core_b)
    padded_k = padded(k_old, (("space", 1),), 1)
    laplace = diffuse(padded_k, face_class)
    cells_total = depth_x * rows_y * cols_z * n_space
    samp_rows = basis_v.shape[1]
    samples_total = samp_rows * n_samp
    lane_width = rank_size // n_space
    full_v = lax.all_gather(basis_v, "space", axis=0, tiled=True)
    k_flat = k_old.reshape(rank_size, -1)
    u_rows = full_u.reshape(rank_size, -1)
    lap_b = laplace.reshape(rank_size, -1).astype(jnp.bfloat16)
    moment_part = lax.dot_general(
        u_rows, lap_b, (((1,), (1,)), ((), ())), preferred_element_type=jnp.float32
    )
    moment = lax.psum(moment_part, "space")
    growth = 0.5 + 0.5 * sample_class.astype(jnp.float32)
    block_rows = min(256, samp_rows)
    block_count = samp_rows // block_rows
    cell_weight = rank_size / cells_total

    def tile_terms(offset):
        v_block = lax.dynamic_slice_in_dim(full_v, offset, block_rows, 1)
        g_block = lax.dynamic_slice_in_dim(growth, offset, block_rows, 0)
        sample_field = lax.dot_general(
            k_flat, v_block, (((0,), (0,)), ((), ())), preferred_element_type=jnp.float32
        )
        reaction = (
            g_block[None, :] * sample_field - sample_field * sample_field * sample_field
        ).astype(jnp.bfloat16)
        onto_v = lax.dot_general(
            v_block, reaction, (((1,), (1,)), ((), ())), preferred_element_type=jnp.float32
        )
        onto_u = lax.dot_general(
            u_rows, reaction, (((1,), (0,)), ((), ())), preferred_element_type=jnp.float32
        )
        return (onto_v, onto_u * cell_weight)

    start_acc = jnp.zeros((rank_size, k_flat.shape[1]), jnp.float32)

    def turn_after(turn_index, state_pair):
        accumulated, l_terms = state_pair
        offset = turn_index * block_rows
        onto_v, l_term = tile_terms(offset)
        l_terms = lax.dynamic_update_slice_in_dim(l_terms, l_term, offset, 1)
        return (accumulated + onto_v, l_terms)

    start_terms = jnp.zeros((rank_size, samp_rows), jnp.float32)
    accumulated, l_terms = lax.fori_loop(0, block_count, turn_after, (start_acc, start_terms))
    l_proj = lax.psum_scatter(l_terms, "space", scatter_dimension=0, tiled=True)
    samp_offset = lax.axis_index("samp") * narrow
    k_term = accumulated.reshape(rank_size, depth_x, rows_y, cols_z)
    k_summed = lax.psum(k_term, "samp")
    k_proj = lax.dynamic_slice_in_dim(k_summed, samp_offset, narrow, 0)
    k_proj = k_proj * (rank_size / samples_total)
    k_mine = lax.dynamic_slice_in_dim(k_old, samp_offset, narrow, 0).astype(jnp.float32)
    lap_mine = lax.dynamic_slice_in_dim(laplace, samp_offset, narrow, 0)
    k_new = k_mine + step_size * (lap_mine + k_proj)
    lane_offset = lax.axis_index("space") * lane_width
    core_rows = lax.dynamic_slice_in_dim(core_b, lane_offset, lane_width, 0)
    l_old = jnp.dot(core_rows, full_v, preferred_element_type=jnp.float32)
    moment_rows = lax.dynamic_slice_in_dim(moment, lane_offset, lane_width, 0) * cell_weight
    side_term = jnp.dot(moment_rows, full_v.astype(jnp.float32), precision=lax.Precision.HIGHEST)
    l_new = l_old + step_size * (side_term + l_proj)
    return (k_new, l_new)


def solution(mesh):
    placed = (
        P("samp", "space", None, None),
        P("space", "samp"),
        P(),
        P(None, "space", None, None),
        P("samp"),
    )
    return jax.shard_map(
        per_device,
        mesh=mesh,
        in_specs=placed,
        out_specs=(P("samp", "space", None, None), P("space", "samp")),
        check_vma=False,
    )
```

profile of v0, /device:TPU:0, one launch (start us, length us, event | category | flops | bytes accessed | tf_op | source)
XLA Modules:
  0.0 497.0 jit_solution(16505963637963926047)
XLA Ops:
  8.8 37.5 %all_gather.6 = bf16[128,2,8,128]{3,2,1,0:T(8,128)(2,1)S(1)} all-gather(bf16[16,2,8,128]{3,2,1,0:T(8,128)(2,1)} %param.7), channel_id=1, replica_groups=mesh['space'=16,'samp'=8] {'samp'}, dimensions={0}, use_global_device_ids=true | all-gather | bytes 589824 | tf_op jit(solution)/shard_map/all_gather | solution.py:59
  49.4 1.3 collective-permute-start.1
  50.6 3.8 collective-permute-start
  55.2 2.4 broadcast_in_dim.11.clone
  57.6 155.9 %while.16 = (s32[]{:T(128)}, f32[128,2048]{1,0:T(8,128)S(1)}, f32[128,8192]{1,0:T(8,128)}, bf16[128,8192]{1,0:T(8,128)(2,1)}, f32[8192]{0:T(1024)}, /*index=5*/b...) while((s32[]{:T(128)}, f32[128,2048]{1,0:T(8,128)S(1)}, ...), condition=%wide.region_1.2_spmd.clone, body=%wide.region_0.1_spmd.clone.sunk | while | flops 405831680 | bytes 7081149 | solution.py:107
  58.4 1.6 fusion.58
  59.9 1.3 convolution_add_fusion.3
  63.2 1.6 fusion.58
  68.1 1.6 fusion.58
  69.7 1.3 convolution_add_fusion.3
  73.0 1.6 fusion.58
  74.6 1.3 convolution_add_fusion.3
  77.9 1.6 fusion.58
  79.5 1.3 convolution_add_fusion.3
  82.8 1.6 fusion.58
  84.4 1.3 convolution_add_fusion.3
  87.6 1.6 fusion.58
  89.2 1.3 convolution_add_fusion.3
  92.5 1.6 fusion.58
  94.1 1.3 convolution_add_fusion.3
  97.4 1.6 fusion.58
  99.0 1.3 convolution_add_fusion.3
  102.3 1.6 fusion.58
  103.9 1.3 convolution_add_fusion.3
  107.1 1.6 fusion.58
  112.0 1.6 fusion.58
  113.6 1.3 convolution_add_fusion.3
  116.8 1.6 fusion.58
  118.4 1.3 convolution_add_fusion.3
  121.7 1.6 fusion.58
  123.3 1.3 convolution_add_fusion.3
  126.6 1.6 fusion.58
  128.2 1.3 convolution_add_fusion.3
  131.4 1.6 fusion.58
  136.3 1.6 fusion.58
  137.9 1.3 convolution_add_fusion.3
  141.2 1.6 fusion.58
  142.8 1.3 convolution_add_fusion.3
  146.0 1.6 fusion.58
  150.9 1.6 fusion.58
  152.5 1.3 convolution_add_fusion.3
  155.8 1.6 fusion.58
  157.4 1.3 convolution_add_fusion.3
  160.6 1.6 fusion.58
  162.2 1.3 convolution_add_fusion.3
  165.5 1.6 fusion.58
  170.4 1.6 fusion.58
  172.0 1.3 convolution_add_fusion.3
  175.2 1.6 fusion.58
  180.1 1.6 fusion.58
  185.0 1.6 fusion.58
  186.6 1.3 convolution_add_fusion.3
  189.8 1.6 fusion.58
  194.7 1.6 fusion.58
  199.6 1.6 fusion.58
  204.5 1.6 fusion.58
  209.3 1.6 fusion.58
  210.9 1.3 convolution_add_fusion.3
  216.0 1.9 fusion.34
  221.6 86.1 %all-reduce.4.cloned.1.call-done = f32[128,2,8,128]{3,2,1,0:T(8,128)} async-done(((f32[128,2,8,128]{3,2,1,0:T(8,128)}), f32[128,2,8,128]{3,2,1,0:T(8,128)}) %all-reduce.4.cloned.1.call-update) | async-done | bytes 1048592 | tf_op jit(solution)/shard_map/psum | solution.py:111
  307.6 1.6 multiply_add_fusion
  309.3 106.7 %all-reduce.6.cloned.1.call-done = f32[128,128]{0,1:T(8,128)} async-done(((f32[128,128]{0,1:T(8,128)}), f32[128,128]{0,1:T(8,128)}) %all-reduce.6.cloned.1.call-update) | async-done | bytes 65552 | tf_op jit(solution)/shard_map/psum | solution.py:74
  416.0 71.8 %reduce-scatter.2.cloned.1.call-done = f32[8,8192]{1,0:T(8,128)} async-done(((f32[128,8192]{1,0:T(8,128)}), f32[8,8192]{1,0:T(8,128)}) %reduce-scatter.2.cloned.1.call-update) | async-done | bytes 262160 | tf_op jit(solution)/shard_map/reduce_scatter | solution.py:108
  487.7 2.7 fusion.8
  (175 shorter events, 88.8 us)
Async XLA Ops:
  7.2 48.0 %all-gather.2.cloned.1.call-start = ((), (), s32[]{:S(2)}) async-start(), calls=%async_computation.1 | async-start | bytes 2228224 | tf_op jit(solution)/shard_map/all_gather | solution.py:67
  7.9 299.7 %all-reduce.4.cloned.1.call-start = ((), (), s32[]{:S(2)}) async-start(), calls=%async_computation.2 | async-start | bytes 2097152 | tf_op jit(solution)/shard_map/psum | solution.py:111
  8.8 38.6 %copy-start.3 = (bf16[128,128]{1,0:T(8,128)(2,1)}, bf16[128,128]{1,0:T(8,128)(2,1)S(1)}, u32[]{:S(2)}) copy-start(bf16[128,128]{1,0:T(8,128)(2,1)S(1)} %convert_element_type.32) | copy-start | bytes 98308
  46.2 8.3 %copy-start.1 = (bf16[128,2,8,128]{3,2,1,0:T(8,128)(2,1)}, bf16[128,2,8,128]{3,2,1,0:T(8,128)(2,1)S(1)}, u32[]{:S(2)}) copy-start(bf16[128,2,8,128]{3,2,1,0:T(8,128)(2,1)S(1)} %all_gather.6) | copy-start | bytes 1572868
  46.2 8.3 %copy-start.5 = (s32[8192]{0:T(1024)S(1)}, s32[8192]{0:T(1024)}, u32[]{:S(2)}) copy-start(s32[8192]{0:T(1024)} %param.11) | copy-start | bytes 98308
  49.4 165.4 %collective-permute-start.1 = (bf16[128,1,8,128]{3,2,1,0:T(8,128)(2,1)}, bf16[128,1,8,128]{3,2,1,0:T(8,128)(2,1)S(1)}, u32[]{:S(2)}, u32[]{:S(2)}) collective-permute-start(bf16[128,1,8,128]{3,2,1,0:T(8,128)(2,1)} %get-tuple-element.170), channel_id=1, source_target_pairs={{8,0},{16,8},{24,16},{32,24},{40,32},{48,40},{56,48},{64,56},{72,6... | collective-permute-start | bytes 786440 | tf_op jit(solution)/shard_map/ppermute | solution.py:19
  50.6 164.1 %collective-permute-start = (bf16[128,1,8,128]{3,2,1,0:T(8,128)(2,1)}, bf16[128,1,8,128]{3,2,1,0:T(8,128)(2,1)}, u32[]{:S(2)}, u32[]{:S(2)}) collective-permute-start(bf16[128,1,8,128]{3,2,1,0:T(8,128)(2,1)} %get-tuple-element.169), channel_id=1, source_target_pairs={{0,8},{8,16},{16,24},{24,32},{32,40},{40,48},{48,56},{56,64},{64,7... | collective-permute-start | bytes 786440 | tf_op jit(solution)/shard_map/ppermute | solution.py:17
  213.5 1.3 copy-start.4
  214.7 201.3 %all-reduce.6.cloned.1.call-start = ((), (), s32[]{:S(2)}) async-start(), calls=%async_computation.3 | async-start | bytes 131072 | tf_op jit(solution)/shard_map/psum | solution.py:74
  216.0 1.9 copy-start.2
  218.9 268.8 %reduce-scatter.2.cloned.1.call-start = ((), (), s32[]{:S(2)}) async-start(), calls=%async_computation.4 | async-start | bytes 4456448 | tf_op jit(solution)/shard_map/reduce_scatter | solution.py:108
  218.9 1.6 copy-start
Sparse Core Ops, SparseCore 0:
  9.7 37.1 all-gather.1
  214.8 92.7 all-reduce.3
  310.7 105.2 all-reduce.5
  418.2 69.4 reduce-scatter.1
where the time goes:
time: 501 us; the launch traced here: 497 us
  waiting for transfers between devices  266 us (53%)
  matrix products  111 us (22%)
  local copies, waits for them, and re-layouts  56 us (11%)
  blocking collectives  37.5 us (7%)
  between operations  13.9 us (3%)
  other arithmetic  6.25 us (1%)
  starting transfers between devices  5.2 us (1%)
    psum x1, waiting for transfers between devices, per_device(): moment = lax.psum(moment_part, 'space')  107 us
    psum x1, waiting for transfers between devices, per_device(): k_summed = lax.psum(k_term, 'samp')  86.1 us
    reduce_scatter x1, waiting for transfers between devices, per_device(): l_proj = lax.psum_scatter(l_terms, 'space', scatter_dimension=0, tiled=True)  71.8 us
    dot_general x32, matrix products, tile_terms(): lax.dot_general(k_flat, v_block, (((0,), (0,)), ((), ())), preferred_elem...  50.6 us
    dot_general x32, matrix products, tile_terms(): lax.dot_general(v_block, reaction, (((1,), (1,)), ((), ())), preferred_el...  40.9 us
    all_gather x1, blocking collectives, per_device(): full_u = lax.all_gather(basis_u, 'samp', axis=0, tiled=True)  37.5 us
    dynamic_update_slice x64, local copies, waits for them, and re-layouts, turn_after(): l_terms = lax.dynamic_update_slice_in_dim(l_terms, l_term, offset, 1)  24.9 us
    dynamic_slice x32, local copies, waits for them, and re-layouts, tile_terms(): g_block = lax.dynamic_slice_in_dim(growth, offset, block_rows, 0)  24.3 us
  transfers between devices with their start and end apart: 6, of which 3 were waited for; matrix products, arithmetic and copies ran while one was open for 34% of the time, Pallas kernels for 0%

commit v1 on v0

--- a/solution.py
+++ b/solution.py
@@ -108,7 +108,8 @@
     l_proj = lax.psum_scatter(l_terms, "space", scatter_dimension=0, tiled=True)
     samp_offset = lax.axis_index("samp") * narrow
     k_term = accumulated.reshape(rank_size, depth_x, rows_y, cols_z)
-    k_summed = lax.psum(k_term, "samp")
+    parts = lax.all_gather(k_term, "samp", axis=0, tiled=False)
+    k_summed = parts.sum(axis=0)
     k_proj = lax.dynamic_slice_in_dim(k_summed, samp_offset, narrow, 0)
     k_proj = k_proj * (rank_size / samples_total)
     k_mine = lax.dynamic_slice_in_dim(k_old, samp_offset, narrow, 0).astype(jnp.float32)

time: 501 us -> 389 us (0.78)
  waiting for transfers between devices: 266 us -> 185 us
  local copies, waits for them, and re-layouts: 56 us -> 33.1 us
  matrix products: 111 us -> 102 us
    psum x1, waiting for transfers between devices: 107 us -> 0.01 us  [per_device(): moment = lax.psum(moment_part, 'space')]
    all_gather x0 -> x1, waiting for transfers between devices: none -> 105 us  [per_device(): parts = lax.all_gather(k_term, 'samp', axis=0, tiled=False)]
    psum x1 -> x0, waiting for transfers between devices: 86.1 us -> none  [per_device(): k_summed = lax.psum(k_term, 'samp')]
    dynamic_slice x32, local copies, waits for them, and re-layouts: 24.3 us -> 2.49 us  [tile_terms(): g_block = lax.dynamic_slice_in_dim(growth, offset, block_rows, 0)]
    dot_general x32, matrix products: 50.6 us -> 42.8 us  [tile_terms(): lax.dot_general(k_flat, v_block, (((0,), (0,)), ((), ())), preferred_elem...]
  transfers between devices with their start and end apart: 6 -> 6, of which waited for: 3 -> 3; matrix products, arithmetic and copies ran while one was open for 34% -> 36% of each run, Pallas kernels for 0% -> 0%
where the time goes in v1:
time: 389 us; the launch traced here: 385 us
  waiting for transfers between devices  185 us (48%)
  matrix products  102 us (26%)
  blocking collectives  37.5 us (10%)
  local copies, waits for them, and re-layouts  33.1 us (9%)
  between operations  13.9 us (4%)
  other arithmetic  9.56 us (2%)
    all_gather x1, waiting for transfers between devices, per_device(): parts = lax.all_gather(k_term, 'samp', axis=0, tiled=False)  105 us
    reduce_scatter x1, waiting for transfers between devices, per_device(): l_proj = lax.psum_scatter(l_terms, 'space', scatter_dimension=0, tiled=True)  75.4 us
    dot_general x32, matrix products, tile_terms(): lax.dot_general(k_flat, v_block, (((0,), (0,)), ((), ())), preferred_elem...  42.8 us
    dot_general x32, matrix products, tile_terms(): lax.dot_general(v_block, reaction, (((1,), (1,)), ((), ())), preferred_el...  40.7 us
    all_gather x1, blocking collectives, per_device(): full_u = lax.all_gather(basis_u, 'samp', axis=0, tiled=True)  37.5 us
    dynamic_update_slice x64, local copies, waits for them, and re-layouts, turn_after(): l_terms = lax.dynamic_update_slice_in_dim(l_terms, l_term, offset, 1)  25.1 us
    dot_general x32, matrix products, tile_terms(): lax.dot_general(u_rows, reaction, (((1,), (0,)), ((), ())), preferred_ele...  13.9 us
  transfers between devices with their start and end apart: 6, of which 3 were waited for; matrix products, arithmetic and copies ran while one was open for 36% of the time, Pallas kernels for 0%

profile of v1, /device:TPU:0, one launch (start us, length us, event | category | flops | bytes accessed | tf_op | source)
XLA Modules:
  0.0 385.4 jit_solution(14308192738715752003)
XLA Ops:
  8.8 37.5 %all_gather.9 = bf16[128,2,8,128]{3,2,1,0:T(8,128)(2,1)S(1)} all-gather(bf16[16,2,8,128]{3,2,1,0:T(8,128)(2,1)} %param.7), channel_id=1, replica_groups=mesh['space'=16,'samp'=8] {'samp'}, dimensions={0}, use_global_device_ids=true | all-gather | bytes 589824 | tf_op jit(solution)/shard_map/all_gather | solution.py:59
  47.6 1.3 collective-permute-start
  48.9 1.3 collective-permute-start.1
  50.4 4.0 %collective-permute-done.1 = bf16[128,1,8,128]{3,2,1,0:T(8,128)(2,1)} collective-permute-done((bf16[128,1,8,128]{3,2,1,0:T(8,128)(2,1)}, bf16[128,1,8,128]{3,2,1,0:T(8,128)(2,1)}, u32[]{:S(2)}, u32[]{:S(2)}) %collective-permute-start.1) | collective-permute-done | bytes 262176 | tf_op jit(solution)/shard_map/ppermute | solution.py:19
  55.7 1.8 fusion.34
  58.6 2.4 broadcast_in_dim.11.clone
  61.0 126.7 %while.16 = (s32[]{:T(128)}, f32[128,2048]{1,0:T(8,128)S(1)}, f32[128,8192]{1,0:T(8,128)}, bf16[128,8192]{1,0:T(8,128)(2,1)}, f32[8192]{0:T(1024)S(1)}, /*index=...) while((s32[]{:T(128)}, f32[128,2048]{1,0:T(8,128)S(1)}, ...), condition=%wide.region_1.2_spmd.clone, body=%wide.region_0.1_spmd.clone.sunk | while | flops 405831680 | bytes 7081141 | solution.py:107
  61.1 1.3 fusion.58
  63.6 1.3 convolution_add_fusion.3
  65.0 1.3 fusion.58
  69.0 1.3 fusion.58
  72.9 1.3 fusion.58
  75.5 1.3 convolution_add_fusion.3
  76.9 1.3 fusion.58
  79.5 1.3 convolution_add_fusion.3
  80.9 1.3 fusion.58
  83.4 1.3 convolution_add_fusion.3
  84.8 1.3 fusion.58
  87.4 1.3 convolution_add_fusion.3
  88.8 1.3 fusion.58
  91.4 1.3 convolution_add_fusion.3
  92.8 1.3 fusion.58
  95.3 1.3 convolution_add_fusion.3
  96.7 1.3 fusion.58
  99.3 1.3 convolution_add_fusion.3
  100.7 1.3 fusion.58
  103.3 1.3 convolution_add_fusion.3
  104.7 1.3 fusion.58
  108.6 1.3 fusion.58
  111.2 1.3 convolution_add_fusion.3
  112.6 1.3 fusion.58
  116.6 1.3 fusion.58
  120.5 1.3 fusion.58
  123.1 1.3 convolution_add_fusion.3
  124.5 1.3 fusion.58
  127.0 1.3 convolution_add_fusion.3
  128.4 1.3 fusion.58
  131.0 1.3 convolution_add_fusion.3
  132.4 1.3 fusion.58
  136.3 1.3 fusion.58
  140.3 1.3 fusion.58
  144.2 1.3 fusion.58
  146.8 1.3 convolution_add_fusion.3
  148.2 1.3 fusion.58
  150.7 1.3 convolution_add_fusion.3
  152.1 1.3 fusion.58
  156.1 1.3 fusion.58
  158.7 1.3 convolution_add_fusion.3
  160.0 1.3 fusion.58
  164.0 1.3 fusion.58
  167.9 1.3 fusion.58
  170.5 1.3 convolution_add_fusion.3
  171.9 1.3 fusion.58
  174.5 1.3 convolution_add_fusion.3
  175.8 1.3 fusion.58
  179.8 1.3 fusion.58
  182.4 1.3 convolution_add_fusion.3
  183.8 1.3 fusion.58
  186.4 1.3 convolution_add_fusion.3
  190.0 75.4 %reduce-scatter.2.cloned.1.call-done = f32[8,8192]{1,0:T(8,128)} async-done(((f32[128,8192]{1,0:T(8,128)}), f32[8,8192]{1,0:T(8,128)}) %reduce-scatter.2.cloned.1.call-update) | async-done | bytes 262160 | tf_op jit(solution)/shard_map/reduce_scatter | solution.py:108
  265.4 2.7 fusion.8
  268.1 105.0 %all-gather.5.cloned.1.call-done = f32[8,128,2,8,128]{4,3,2,1,0:T(8,128)} async-done(((f32[1,128,2,8,128]{4,3,2,1,0:T(8,128)}), f32[8,128,2,8,128]{4,3,2,1,0:T(8,128)}) %all-gather.5.cloned.1.call-update) | async-done | bytes 8388624 | tf_op jit(solution)/shard_map/all_gather | solution.py:111
  373.2 4.1 %reduce_sum.9 = f32[128,2,8,128]{3,2,1,0:T(8,128)S(1)} reduce(f32[8,128,2,8,128]{4,3,2,1,0:T(8,128)} %all-gather.5.cloned.1.call-done, f32[]{:T(128)} %constant.61.clone.1), dimensions={0}, to_apply=%region_2.3 | reduce | flops 1835008 | bytes 9437188 | tf_op jit(solution)/shard_map/reduce_sum | solution.py:112
  377.2 1.6 multiply_add_fusion
  (172 shorter events, 64.4 us)
Async XLA Ops:
  7.2 43.0 %copy-start.2 = (s32[6,2,8,128]{3,2,1,0:T(8,128)S(1)}, s32[6,2,8,128]{3,2,1,0:T(8,128)}, u32[]{:S(2)}) copy-start(s32[6,2,8,128]{3,2,1,0:T(8,128)} %param.10) | copy-start | bytes 147460
  7.2 51.4 %all-gather.3.cloned.1.call-start = ((), (), s32[]{:S(2)}) async-start(), calls=%async_computation.1 | async-start | bytes 2228224 | tf_op jit(solution)/shard_map/all_gather | solution.py:67
  7.9 182.1 %all-reduce.3.cloned.1.call-start = ((), (), s32[]{:S(2)}) async-start(), calls=%async_computation.3 | async-start | bytes 131072 | tf_op jit(solution)/shard_map/psum | solution.py:74
  46.3 4.1 %copy-start.3 = (s32[8192]{0:T(1024)S(1)}, s32[8192]{0:T(1024)}, u32[]{:S(2)}) copy-start(s32[8192]{0:T(1024)} %param.11) | copy-start | bytes 98308
  46.7 9.0 %copy-start.1 = (bf16[16,8,16,128]{3,2,1,0:T(8,128)(2,1)}, bf16[16,8,16,128]{3,2,1,0:T(8,128)(2,1)S(1)}, u32[]{:S(2)}) copy-start(bf16[16,8,16,128]{3,2,1,0:T(8,128)(2,1)S(1)} %copy.17) | copy-start | bytes 1572868
  47.6 2.8 collective-permute-start
  48.9 5.6 %collective-permute-start.1 = (bf16[128,1,8,128]{3,2,1,0:T(8,128)(2,1)}, bf16[128,1,8,128]{3,2,1,0:T(8,128)(2,1)}, u32[]{:S(2)}, u32[]{:S(2)}) collective-permute-start(bf16[128,1,8,128]{3,2,1,0:T(8,128)(2,1)} %get-tuple-element.170), channel_id=1, source_target_pairs={{8,0},{16,8},{24,16},{32,24},{40,32},{48,40},{56,48},{64,56},{72,6... | collective-permute-start | bytes 786440 | tf_op jit(solution)/shard_map/ppermute | solution.py:19
  58.5 206.9 %reduce-scatter.2.cloned.1.call-start = ((), (), s32[]{:S(2)}) async-start(), calls=%async_computation.4 | async-start | bytes 4456448 | tf_op jit(solution)/shard_map/reduce_scatter | solution.py:108
  187.7 2.0 copy-start
  187.7 185.5 %all-gather.5.cloned.1.call-start = ((), (), s32[]{:S(2)}) async-start(), calls=%async_computation.2 | async-start | bytes 9437184 | tf_op jit(solution)/shard_map/all_gather | solution.py:111
Sparse Core Ops, SparseCore 0:
  9.7 37.1 all-gather.2
  58.6 114.0 all-reduce.2
  187.8 77.5 reduce-scatter.1
  267.6 105.5 all-gather.4
